TPU v7x, 1024 devices: a whole 4x8x16 slice. The times are simulated.
1024 devices in a mesh: gx: 32 (over y, x), gy: 16 (over z), gz: 2 (over core).
Axes of the slice: x: 4, y: 8, z: 16, core: 2. Of those that a mesh axis runs over, the one named last changes fastest.
Arguments:
- s_blocks: bfloat16 [1024, 4, 128, 128], P(('gx', 'gy', 'gz')), may hold values from -1 to 2
- s_columns: int32 [1024, 4], P(('gx', 'gy', 'gz')), may hold values from 0 to 6, as said below
- new_home: int32 [1024], P(('gx', 'gy', 'gz')), may hold values from 0 to 1, as said below
- z_pattern: int32 [1024, 7], P(('gx', 'gy', 'gz')), may hold values 0 or 1
- y_pattern: int32 [1024, 7], P(('gx', 'gy', 'gz')), may hold values 0 or 1
Outputs:
- z_out: bfloat16 [1024, 128, 7, 128], P(('gx', 'gy', 'gz'))
- y_out: bfloat16 [1024, 128, 7, 128], P(('gx', 'gy', 'gz'))
Inputs may be any that keep to these rules, and one draw needn't show every extreme that they name: new_home = 1 * (new gz index) + new slot; among the clusters of devices that share gx and gy indices each value occurs once, and the 1 clusters of one device go to 1 different devices. `s_columns`: the entries of a row are distinct, and the first is the cluster's own diagonal block in the new layout (part 0, its new slot).
All inputs are finite; a program needn't handle non-finite values. No bound on the sum of `z_pattern` or of `y_pattern` on one device may be relied on, other than what follows from the above.
Results may differ from a plain program's by a relative error of at most 0.0058.
Values may be sent and summed in bfloat16 or wider, within the bound.
A program may use at most 32 MiB of HBM per device.

v0:
```python
import jax
import jax.numpy as jnp
from jax import lax
from jax.sharding import PartitionSpec as P


def from_behind(x, axis, by):
    count = lax.axis_size(axis)
    pairs = [(i, i + by) for i in range(count) if 0 <= i + by < count]
    return lax.ppermute(x, axis, pairs)


def expand(retain, matrix):
    slot_count = retain.shape[0]
    block_size = matrix.shape[0] // slot_count
    blocked = matrix.reshape(slot_count, block_size, 7, slot_count, block_size)
    chosen = jnp.where(retain[:, None, :, :, None], blocked, jnp.zeros((), matrix.dtype))
    return chosen.reshape(matrix.shape)


def block_product(left, right, halo):
    rows_total = left.shape[0]
    stacked = jnp.concatenate([right[:, 0, :][None], halo[:, :, 1, :]], axis=0).reshape(
        7 * rows_total, rows_total
    )
    own_column = jnp.dot(
        left.reshape(rows_total, 7 * rows_total), stacked, preferred_element_type=jnp.float32
    )
    across = jnp.dot(
        left[:, 0, :],
        right[:, 1:, :].reshape(rows_total, 6 * rows_total),
        preferred_element_type=jnp.float32,
    ).reshape(rows_total, 6, rows_total)
    across = across + jnp.einsum(
        "irj,rjk->irk", left[:, 1:, :], halo[:, :, 0, :], preferred_element_type=jnp.float32
    )
    return jnp.concatenate([own_column[:, None, :], across], axis=1)


def gather_halo(matrices):

    def packed(facing):
        return jnp.stack(
            [matrix[:, which_block, :] for matrix in matrices for which_block in (0, facing)],
            axis=1,
        )

    arrived = {}
    for offset in (1, -1):
        arrived["x", offset] = from_behind(packed(2 if offset == 1 else 1), "gx", offset)
    for offset in (1, -1):
        arrived["y", offset] = from_behind(packed(4 if offset == 1 else 3), "gy", offset)
    for offset in (1, -1):
        arrived["z", offset] = from_behind(packed(6 if offset == 1 else 5), "gz", offset)
    ordered = [
        arrived["x", 1],
        arrived["x", -1],
        arrived["y", 1],
        arrived["y", -1],
        arrived["z", 1],
        arrived["z", -1],
    ]
    return jnp.stack(ordered, axis=0)


def body(s_blocks, s_columns, new_home, z_pattern, y_pattern):
    slot_count = s_blocks.shape[0]
    block_count = s_blocks.shape[1]
    block_size = s_blocks.shape[2]
    rows_total = slot_count * block_size
    lanes = lax.axis_size("gz")
    targets = jnp.arange(lanes, dtype=jnp.int32)
    dest_device = new_home // slot_count
    dest_slot = new_home % slot_count
    chosen = dest_device[None, :] == targets[:, None]
    outgoing = jnp.einsum(
        "tj,jkab->tkab", chosen.astype(jnp.bfloat16), s_blocks, preferred_element_type=jnp.float32
    ).astype(jnp.bfloat16)
    labels = jnp.concatenate(
        [s_columns, dest_slot[:, None], jnp.ones((slot_count, 1), jnp.int32)], axis=1
    )
    label_out = jnp.sum(jnp.where(chosen[:, :, None], labels[None], 0), axis=1)
    arrived_blocks, arrived_labels = (
        lax.all_to_all(outgoing, "gz", split_axis=0, concat_axis=0, tiled=True),
        lax.all_to_all(label_out, "gz", split_axis=0, concat_axis=0, tiled=True),
    )
    present = arrived_labels[:, block_count + 1] == 1
    landing = arrived_labels[:, block_count]
    column_of = arrived_labels[:, :block_count]
    column_ids = jnp.arange(7 * slot_count, dtype=jnp.int32)
    slot_ids = jnp.arange(slot_count, dtype=jnp.int32)
    routing = (
        present[None, None, :, None]
        & (landing[None, None, :, None] == slot_ids[:, None, None, None])
        & (column_of[None, None, :, :] == column_ids[None, :, None, None])
    )
    dense = jnp.einsum(
        "qcsk,skab->qacb",
        routing.astype(jnp.bfloat16),
        arrived_blocks,
        preferred_element_type=jnp.float32,
    ).astype(jnp.bfloat16)
    start = dense.reshape(rows_total, 7, rows_total)
    place_x = lax.axis_index("gx")
    place_y = lax.axis_index("gy")
    place_z = lax.axis_index("gz")
    valid = jnp.stack(
        [
            place_x >= 0,
            place_x > 0,
            place_x < lax.axis_size("gx") - 1,
            place_y > 0,
            place_y < lax.axis_size("gy") - 1,
            place_z > 0,
            place_z < lanes - 1,
        ]
    )
    diagonal = (jnp.arange(7)[None, :, None] == 0) & (
        slot_ids[:, None, None] == slot_ids[None, None, :]
    )
    retain_valid = valid[None, :, None]
    retain_y = ((y_pattern.reshape(slot_count, 7, slot_count) == 1) | diagonal) & valid[
        None, :, None
    ]
    retain_z = ((z_pattern.reshape(slot_count, 7, slot_count) == 1) | diagonal) & valid[
        None, :, None
    ]
    identity = jnp.concatenate(
        [
            jnp.eye(rows_total, dtype=jnp.float32)[:, None, :],
            jnp.zeros((rows_total, 6, rows_total), jnp.float32),
        ],
        axis=1,
    )
    square = expand(retain_valid, start)
    middle = expand(retain_y, 1.5 * identity - 0.5 * square.astype(jnp.float32)).astype(
        jnp.bfloat16
    )
    halo_middle = gather_halo([middle])
    square_next = expand(retain_y, block_product(square, middle, halo_middle)).astype(jnp.bfloat16)
    inverse = expand(retain_z, middle)
    square = square_next
    both_halos = gather_halo([square, inverse])
    halo_square = both_halos[:, :, 0:2, :]
    halo_inverse = both_halos[:, :, 2:4, :]
    quad = expand(retain_y, block_product(inverse, square, halo_square))
    middle = expand(retain_y, 1.5 * identity - 0.5 * quad).astype(jnp.bfloat16)
    halo_middle = gather_halo([middle])
    square_next = expand(retain_y, block_product(square, middle, halo_middle)).astype(jnp.bfloat16)
    inverse = expand(retain_z, block_product(middle, inverse, halo_inverse)).astype(jnp.bfloat16)
    out_shape = (slot_count, block_size, 7 * slot_count, block_size)
    return (inverse.reshape(out_shape), square_next.reshape(out_shape))


def solution(mesh):
    in_specs = (
        P(("gx", "gy", "gz"), None, None, None),
        P(("gx", "gy", "gz"), None),
        P(("gx", "gy", "gz")),
        P(("gx", "gy", "gz"), None),
        P(("gx", "gy", "gz"), None),
    )
    out_specs = (P(("gx", "gy", "gz"), None, None, None), P(("gx", "gy", "gz"), None, None, None))
    return jax.shard_map(body, mesh=mesh, in_specs=in_specs, out_specs=out_specs, check_vma=False)
```

profile of v0, /device:TPU:480, one launch (start us, length us, event | category | flops | bytes accessed | tf_op | source)
XLA Modules:
  0.0 96.2 jit_solution(5230866095804400319)
XLA Ops:
  1.3 0.6 copy-done.6
  2.0 0.6 broadcast_select_fusion.1
  2.6 3.2 %all-to-all-start.1 = ((s32[2,1,6]{2,1,0:T(1,128)}), s32[2,1,6]{2,1,0:T(1,128)S(1)}, u32[]{:S(2)}, u32[]{:S(2)}) async-start(s32[2,1,6]{2,1,0:T(1,128)} %broadcast_select_fusion.1), calls=%async_computation.1 | async-start | bytes 2048 | tf_op jit(solution)/shard_map/all_to_all | solution.py:85
  6.0 0.9 bitcast_convert_fusion
  7.1 0.9 multiply_convert_fusion
  7.9 3.4 %all-to-all-start = ((bf16[2,4,128,128]{3,1,2,0:T(4,128)(2,1)}), bf16[2,4,128,128]{3,1,2,0:T(4,128)(2,1)S(1)}, u32[]{:S(2)}, u32[]{:S(2)}) async-start(bf16[2,4,128,128]{3,1,2,0:T(4,128)(2,1)} %multiply_convert_fusion), calls=%async_computation | async-start | bytes 524288 | tf_op jit(solution)/shard_map/all_to_all | solution.py:84
  11.7 0.5 copy-done.4
  12.3 0.7 all-to-all-done
  12.9 0.5 broadcast_select_fusion
  13.4 0.3 fusion.76
  13.7 0.5 pad_maximum_fusion.16
  14.3 3.4 %collective-permute-start = (bf16[128,2,128]{2,1,0:T(2,128)(2,1)S(1)}, bf16[128,2,128]{2,1,0:T(2,128)(2,1)S(1)}, u32[]{:S(2)}, u32[]{:S(2)}) collective-permute-start(bf16[128,2,128]{2,1,0:T(2,128)(2,1)S(1)} %get-tuple-element.50), channel_id=1, source_target_pairs={{0,32},{32,64},{64,96},{96,128},{128,160},{160,192},{192,224},{224... | collective-permute-start | bytes 196616 | tf_op jit(solution)/shard_map/ppermute | solution.py:10
  17.7 5.8 %collective-permute-start.1 = (bf16[128,2,128]{2,1,0:T(2,128)(2,1)S(1)}, bf16[128,2,128]{2,1,0:T(2,128)(2,1)S(1)}, u32[]{:S(2)}, u32[]{:S(2)}) collective-permute-start(bf16[128,2,128]{2,1,0:T(2,128)(2,1)S(1)} %stack.189), channel_id=1, source_target_pairs={{32,0},{64,32},{96,64},{128,96},{160,128},{192,160},{224,192},{256... | collective-permute-start | bytes 196616 | tf_op jit(solution)/shard_map/ppermute | solution.py:10
  23.5 5.5 %collective-permute-start.2 = (bf16[128,2,128]{2,1,0:T(2,128)(2,1)S(1)}, bf16[128,2,128]{2,1,0:T(2,128)(2,1)S(1)}, u32[]{:S(2)}, u32[]{:S(2)}) collective-permute-start(bf16[128,2,128]{2,1,0:T(2,128)(2,1)S(1)} %get-tuple-element.47), channel_id=1, source_target_pairs={{0,2},{2,4},{4,6},{6,8},{8,10},{10,12},{12,14},{14,16},{16,18},{18... | collective-permute-start | bytes 196616 | tf_op jit(solution)/shard_map/ppermute | solution.py:10
  29.0 1.9 %collective-permute-start.3 = (bf16[128,2,128]{2,1,0:T(2,128)(2,1)S(1)}, bf16[128,2,128]{2,1,0:T(2,128)(2,1)S(1)}, u32[]{:S(2)}, u32[]{:S(2)}) collective-permute-start(bf16[128,2,128]{2,1,0:T(2,128)(2,1)S(1)} %get-tuple-element.48), channel_id=1, source_target_pairs={{2,0},{4,2},{6,4},{8,6},{10,8},{12,10},{14,12},{16,14},{18,16},{20... | collective-permute-start | bytes 196616 | tf_op jit(solution)/shard_map/ppermute | solution.py:10
  30.9 1.3 %collective-permute-start.4 = (bf16[128,2,128]{2,1,0:T(2,128)(2,1)S(1)}, bf16[128,2,128]{2,1,0:T(2,128)(2,1)S(1)}, u32[]{:S(2)}, u32[]{:S(2)}) collective-permute-start(bf16[128,2,128]{2,1,0:T(2,128)(2,1)S(1)} %get-tuple-element.49), channel_id=1, source_target_pairs={{0,1},{2,3},{4,5},{6,7},{8,9},{10,11},{12,13},{14,15},{16,17},{18,... | collective-permute-start | bytes 196616 | tf_op jit(solution)/shard_map/ppermute | solution.py:10
  32.6 0.3 fusion.75
  34.1 0.6 copy.255
  34.7 1.3 %collective-permute-start.5 = (bf16[128,2,128]{2,1,0:T(2,128)(2,1)S(1)}, bf16[128,2,128]{2,1,0:T(2,128)(2,1)S(1)}, u32[]{:S(2)}, u32[]{:S(2)}) collective-permute-start(bf16[128,2,128]{2,1,0:T(2,128)(2,1)S(1)} %get-tuple-element.46), channel_id=1, source_target_pairs={{1,0},{3,2},{5,4},{7,6},{9,8},{11,10},{13,12},{15,14},{17,16},{19,... | collective-permute-start | bytes 196616 | tf_op jit(solution)/shard_map/ppermute | solution.py:10
  36.5 1.3 %collective-permute-done.5 = bf16[128,2,128]{2,1,0:T(2,128)(2,1)S(1)} collective-permute-done((bf16[128,2,128]{2,1,0:T(2,128)(2,1)S(1)}, bf16[128,2,128]{2,1,0:T(2,128)(2,1)S(1)}, u32[]{:S(2)}, u32[]{:S(2)}) %collective-permute-start.5) | collective-permute-done | bytes 65568 | tf_op jit(solution)/shard_map/ppermute | solution.py:10
  37.9 0.6 fusion.72
  39.6 0.3 fusion.74
  39.9 0.4 copy-done
  40.5 0.9 fusion.49
  41.5 5.1 %collective-permute-start.8 = (bf16[128,4,128]{2,1,0:T(4,128)(2,1)S(1)}, bf16[128,4,128]{2,1,0:T(4,128)(2,1)S(1)}, u32[]{:S(2)}, u32[]{:S(2)}) collective-permute-start(bf16[128,4,128]{2,1,0:T(4,128)(2,1)S(1)} %get-tuple-element.38), channel_id=1, source_target_pairs={{0,2},{2,4},{4,6},{6,8},{8,10},{10,12},{12,14},{14,16},{16,18},{18... | collective-permute-start | bytes 393224 | tf_op jit(solution)/shard_map/ppermute | solution.py:10
  46.6 0.3 fusion.45
  46.9 1.9 %collective-permute-start.6 = (bf16[128,4,128]{2,1,0:T(4,128)(2,1)S(1)}, bf16[128,4,128]{2,1,0:T(4,128)(2,1)S(1)}, u32[]{:S(2)}, u32[]{:S(2)}) collective-permute-start(bf16[128,4,128]{2,1,0:T(4,128)(2,1)S(1)} %fusion.45), channel_id=1, source_target_pairs={{0,32},{32,64},{64,96},{96,128},{128,160},{160,192},{192,224},{224... | collective-permute-start | bytes 393224 | tf_op jit(solution)/shard_map/ppermute | solution.py:10
  49.0 7.2 %collective-permute-start.7 = (bf16[128,4,128]{2,1,0:T(4,128)(2,1)S(1)}, bf16[128,4,128]{2,1,0:T(4,128)(2,1)S(1)}, u32[]{:S(2)}, u32[]{:S(2)}) collective-permute-start(bf16[128,4,128]{2,1,0:T(4,128)(2,1)S(1)} %pad_maximum_fusion.11), channel_id=1, source_target_pairs={{32,0},{64,32},{96,64},{128,96},{160,128},{192,160},{224,192},{256... | collective-permute-start | bytes 393224 | tf_op jit(solution)/shard_map/ppermute | solution.py:10
  56.3 1.9 %collective-permute-start.9 = (bf16[128,4,128]{2,1,0:T(4,128)(2,1)S(1)}, bf16[128,4,128]{2,1,0:T(4,128)(2,1)S(1)}, u32[]{:S(2)}, u32[]{:S(2)}) collective-permute-start(bf16[128,4,128]{2,1,0:T(4,128)(2,1)S(1)} %get-tuple-element.39), channel_id=1, source_target_pairs={{2,0},{4,2},{6,4},{8,6},{10,8},{12,10},{14,12},{16,14},{18,16},{20... | collective-permute-start | bytes 393224 | tf_op jit(solution)/shard_map/ppermute | solution.py:10
  58.2 1.3 %collective-permute-start.10 = (bf16[128,4,128]{2,1,0:T(4,128)(2,1)S(1)}, bf16[128,4,128]{2,1,0:T(4,128)(2,1)S(1)}, u32[]{:S(2)}, u32[]{:S(2)}) collective-permute-start(bf16[128,4,128]{2,1,0:T(4,128)(2,1)S(1)} %get-tuple-element.40), channel_id=1, source_target_pairs={{0,1},{2,3},{4,5},{6,7},{8,9},{10,11},{12,13},{14,15},{16,17},{18,... | collective-permute-start | bytes 393224 | tf_op jit(solution)/shard_map/ppermute | solution.py:10
  60.2 1.5 %collective-permute-start.11 = (bf16[128,4,128]{2,1,0:T(4,128)(2,1)S(1)}, bf16[128,4,128]{2,1,0:T(4,128)(2,1)S(1)}, u32[]{:S(2)}, u32[]{:S(2)}) collective-permute-start(bf16[128,4,128]{2,1,0:T(4,128)(2,1)S(1)} %get-tuple-element.37), channel_id=1, source_target_pairs={{1,0},{3,2},{5,4},{7,6},{9,8},{11,10},{13,12},{15,14},{17,16},{19,... | collective-permute-start | bytes 393224 | tf_op jit(solution)/shard_map/ppermute | solution.py:10
  61.9 2.5 %collective-permute-done.9 = bf16[128,4,128]{2,1,0:T(4,128)(2,1)S(1)} collective-permute-done((bf16[128,4,128]{2,1,0:T(4,128)(2,1)S(1)}, bf16[128,4,128]{2,1,0:T(4,128)(2,1)S(1)}, u32[]{:S(2)}, u32[]{:S(2)}) %collective-permute-start.9) | collective-permute-done | bytes 131104 | tf_op jit(solution)/shard_map/ppermute | solution.py:10
  64.5 1.6 %fusion.70 = (bf16[6,128,1,128]{3,2,1,0:T(2,128)(2,1)S(1)}, bf16[6,128,1,128]{3,2,1,0:T(2,128)(2,1)S(1)}, bf16[6,128,1,128]{3,2,1,0:T(2,128)(2,1)S(1)}, bf16[6,128,1,128]{3,2,1,0:T(2,128)(2,1)S(1)}) fusion(bf16[6,128,4,128]{3,2,1,0:T(4,128)(2,1)S(1)} %bitcast_dynamic-update-slice_fusion), kind=kLoop, calls=%fused_computation.141 | loop fusion | bytes 1572864 | tf_op jit(solution)/shard_map/slice | solution.py:23
  66.1 0.9 copy.186
  67.6 0.7 copy-done.2
  69.4 0.5 pad_maximum_fusion.21
  70.0 1.9 %collective-permute-start.12 = (bf16[128,2,128]{2,1,0:T(2,128)(2,1)S(1)}, bf16[128,2,128]{2,1,0:T(2,128)(2,1)S(1)}, u32[]{:S(2)}, u32[]{:S(2)}) collective-permute-start(bf16[128,2,128]{2,1,0:T(2,128)(2,1)S(1)} %get-tuple-element.45), channel_id=1, source_target_pairs={{0,32},{32,64},{64,96},{96,128},{128,160},{160,192},{192,224},{224... | collective-permute-start | bytes 196616 | tf_op jit(solution)/shard_map/ppermute | solution.py:10
  72.4 0.7 copy-done.3
  73.6 0.8 fusion.11
  74.4 7.2 %collective-permute-start.13 = (bf16[128,2,128]{2,1,0:T(2,128)(2,1)S(1)}, bf16[128,2,128]{2,1,0:T(2,128)(2,1)S(1)}, u32[]{:S(2)}, u32[]{:S(2)}) collective-permute-start(bf16[128,2,128]{2,1,0:T(2,128)(2,1)S(1)} %stack.190), channel_id=1, source_target_pairs={{32,0},{64,32},{96,64},{128,96},{160,128},{192,160},{224,192},{256... | collective-permute-start | bytes 196616 | tf_op jit(solution)/shard_map/ppermute | solution.py:10
  81.7 4.1 %collective-permute-start.14 = (bf16[128,2,128]{2,1,0:T(2,128)(2,1)S(1)}, bf16[128,2,128]{2,1,0:T(2,128)(2,1)S(1)}, u32[]{:S(2)}, u32[]{:S(2)}) collective-permute-start(bf16[128,2,128]{2,1,0:T(2,128)(2,1)S(1)} %get-tuple-element.42), channel_id=1, source_target_pairs={{0,2},{2,4},{4,6},{6,8},{8,10},{10,12},{12,14},{14,16},{16,18},{18... | collective-permute-start | bytes 196616 | tf_op jit(solution)/shard_map/ppermute | solution.py:10
  85.8 1.9 %collective-permute-start.15 = (bf16[128,2,128]{2,1,0:T(2,128)(2,1)S(1)}, bf16[128,2,128]{2,1,0:T(2,128)(2,1)S(1)}, u32[]{:S(2)}, u32[]{:S(2)}) collective-permute-start(bf16[128,2,128]{2,1,0:T(2,128)(2,1)S(1)} %get-tuple-element.43), channel_id=1, source_target_pairs={{2,0},{4,2},{6,4},{8,6},{10,8},{12,10},{14,12},{16,14},{18,16},{20... | collective-permute-start | bytes 196616 | tf_op jit(solution)/shard_map/ppermute | solution.py:10
  87.7 1.3 %collective-permute-start.16 = (bf16[128,2,128]{2,1,0:T(2,128)(2,1)S(1)}, bf16[128,2,128]{2,1,0:T(2,128)(2,1)S(1)}, u32[]{:S(2)}, u32[]{:S(2)}) collective-permute-start(bf16[128,2,128]{2,1,0:T(2,128)(2,1)S(1)} %get-tuple-element.44), channel_id=1, source_target_pairs={{0,1},{2,3},{4,5},{6,7},{8,9},{10,11},{12,13},{14,15},{16,17},{18,... | collective-permute-start | bytes 196616 | tf_op jit(solution)/shard_map/ppermute | solution.py:10
  89.0 1.3 %collective-permute-start.17 = (bf16[128,2,128]{2,1,0:T(2,128)(2,1)S(1)}, bf16[128,2,128]{2,1,0:T(2,128)(2,1)S(1)}, u32[]{:S(2)}, u32[]{:S(2)}) collective-permute-start(bf16[128,2,128]{2,1,0:T(2,128)(2,1)S(1)} %get-tuple-element.41), channel_id=1, source_target_pairs={{1,0},{3,2},{5,4},{7,6},{9,8},{11,10},{13,12},{15,14},{17,16},{19,... | collective-permute-start | bytes 196616 | tf_op jit(solution)/shard_map/ppermute | solution.py:10
  90.5 2.6 %collective-permute-done.15 = bf16[128,2,128]{2,1,0:T(2,128)(2,1)S(1)} collective-permute-done((bf16[128,2,128]{2,1,0:T(2,128)(2,1)S(1)}, bf16[128,2,128]{2,1,0:T(2,128)(2,1)S(1)}, u32[]{:S(2)}, u32[]{:S(2)}) %collective-permute-start.15) | collective-permute-done | bytes 65568 | tf_op jit(solution)/shard_map/ppermute | solution.py:10
  93.4 0.6 fusion.71
  94.0 0.9 copy-done.1
  95.4 0.8 fusion.12
  (96 shorter events, 8.6 us)
Async XLA Ops:
  1.3 0.7 copy-start.6
  2.6 5.3 %all-to-all-start.1 = ((s32[2,1,6]{2,1,0:T(1,128)}), s32[2,1,6]{2,1,0:T(1,128)S(1)}, u32[]{:S(2)}, u32[]{:S(2)}) async-start(s32[2,1,6]{2,1,0:T(1,128)} %broadcast_select_fusion.1), calls=%async_computation.1 | async-start | bytes 2048 | tf_op jit(solution)/shard_map/all_to_all | solution.py:85
  7.9 5.0 %all-to-all-start = ((bf16[2,4,128,128]{3,1,2,0:T(4,128)(2,1)}), bf16[2,4,128,128]{3,1,2,0:T(4,128)(2,1)S(1)}, u32[]{:S(2)}, u32[]{:S(2)}) async-start(bf16[2,4,128,128]{3,1,2,0:T(4,128)(2,1)} %multiply_convert_fusion), calls=%async_computation | async-start | bytes 524288 | tf_op jit(solution)/shard_map/all_to_all | solution.py:84
  11.6 0.7 copy-start.4
  11.6 0.7 copy-start.5
  14.3 20.4 %collective-permute-start = (bf16[128,2,128]{2,1,0:T(2,128)(2,1)S(1)}, bf16[128,2,128]{2,1,0:T(2,128)(2,1)S(1)}, u32[]{:S(2)}, u32[]{:S(2)}) collective-permute-start(bf16[128,2,128]{2,1,0:T(2,128)(2,1)S(1)} %get-tuple-element.50), channel_id=1, source_target_pairs={{0,32},{32,64},{64,96},{96,128},{128,160},{160,192},{192,224},{224... | collective-permute-start | bytes 196616 | tf_op jit(solution)/shard_map/ppermute | solution.py:10
  17.7 18.3 %collective-permute-start.1 = (bf16[128,2,128]{2,1,0:T(2,128)(2,1)S(1)}, bf16[128,2,128]{2,1,0:T(2,128)(2,1)S(1)}, u32[]{:S(2)}, u32[]{:S(2)}) collective-permute-start(bf16[128,2,128]{2,1,0:T(2,128)(2,1)S(1)} %stack.189), channel_id=1, source_target_pairs={{32,0},{64,32},{96,64},{128,96},{160,128},{192,160},{224,192},{256... | collective-permute-start | bytes 196616 | tf_op jit(solution)/shard_map/ppermute | solution.py:10
  23.5 12.6 %collective-permute-start.2 = (bf16[128,2,128]{2,1,0:T(2,128)(2,1)S(1)}, bf16[128,2,128]{2,1,0:T(2,128)(2,1)S(1)}, u32[]{:S(2)}, u32[]{:S(2)}) collective-permute-start(bf16[128,2,128]{2,1,0:T(2,128)(2,1)S(1)} %get-tuple-element.47), channel_id=1, source_target_pairs={{0,2},{2,4},{4,6},{6,8},{8,10},{10,12},{12,14},{14,16},{16,18},{18... | collective-permute-start | bytes 196616 | tf_op jit(solution)/shard_map/ppermute | solution.py:10
  29.0 7.4 %collective-permute-start.3 = (bf16[128,2,128]{2,1,0:T(2,128)(2,1)S(1)}, bf16[128,2,128]{2,1,0:T(2,128)(2,1)S(1)}, u32[]{:S(2)}, u32[]{:S(2)}) collective-permute-start(bf16[128,2,128]{2,1,0:T(2,128)(2,1)S(1)} %get-tuple-element.48), channel_id=1, source_target_pairs={{2,0},{4,2},{6,4},{8,6},{10,8},{12,10},{14,12},{16,14},{18,16},{20... | collective-permute-start | bytes 196616 | tf_op jit(solution)/shard_map/ppermute | solution.py:10
  30.9 5.5 %collective-permute-start.4 = (bf16[128,2,128]{2,1,0:T(2,128)(2,1)S(1)}, bf16[128,2,128]{2,1,0:T(2,128)(2,1)S(1)}, u32[]{:S(2)}, u32[]{:S(2)}) collective-permute-start(bf16[128,2,128]{2,1,0:T(2,128)(2,1)S(1)} %get-tuple-element.49), channel_id=1, source_target_pairs={{0,1},{2,3},{4,5},{6,7},{8,9},{10,11},{12,13},{14,15},{16,17},{18,... | collective-permute-start | bytes 196616 | tf_op jit(solution)/shard_map/ppermute | solution.py:10
  34.7 3.1 %collective-permute-start.5 = (bf16[128,2,128]{2,1,0:T(2,128)(2,1)S(1)}, bf16[128,2,128]{2,1,0:T(2,128)(2,1)S(1)}, u32[]{:S(2)}, u32[]{:S(2)}) collective-permute-start(bf16[128,2,128]{2,1,0:T(2,128)(2,1)S(1)} %get-tuple-element.46), channel_id=1, source_target_pairs={{1,0},{3,2},{5,4},{7,6},{9,8},{11,10},{13,12},{15,14},{17,16},{19,... | collective-permute-start | bytes 196616 | tf_op jit(solution)/shard_map/ppermute | solution.py:10
  39.6 0.7 copy-start
  41.5 20.3 %collective-permute-start.8 = (bf16[128,4,128]{2,1,0:T(4,128)(2,1)S(1)}, bf16[128,4,128]{2,1,0:T(4,128)(2,1)S(1)}, u32[]{:S(2)}, u32[]{:S(2)}) collective-permute-start(bf16[128,4,128]{2,1,0:T(4,128)(2,1)S(1)} %get-tuple-element.38), channel_id=1, source_target_pairs={{0,2},{2,4},{4,6},{6,8},{8,10},{10,12},{12,14},{14,16},{16,18},{18... | collective-permute-start | bytes 393224 | tf_op jit(solution)/shard_map/ppermute | solution.py:10
  46.6 2.3 %slice-start = ((bf16[128,7,128]{2,1,0:T(8,128)(2,1)}), bf16[128,2,128]{2,1,0:T(2,128)(2,1)S(1)}, s32[]{:S(2)}) async-start(bf16[128,7,128]{2,1,0:T(8,128)(2,1)} %copy-done), calls=%async_computation.2 | async-start | bytes 131072 | tf_op jit(solution)/shard_map/slice | solution.py:23
  46.9 13.2 %collective-permute-start.6 = (bf16[128,4,128]{2,1,0:T(4,128)(2,1)S(1)}, bf16[128,4,128]{2,1,0:T(4,128)(2,1)S(1)}, u32[]{:S(2)}, u32[]{:S(2)}) collective-permute-start(bf16[128,4,128]{2,1,0:T(4,128)(2,1)S(1)} %fusion.45), channel_id=1, source_target_pairs={{0,32},{32,64},{64,96},{96,128},{128,160},{160,192},{192,224},{224... | collective-permute-start | bytes 393224 | tf_op jit(solution)/shard_map/ppermute | solution.py:10
  49.0 12.7 %collective-permute-start.7 = (bf16[128,4,128]{2,1,0:T(4,128)(2,1)S(1)}, bf16[128,4,128]{2,1,0:T(4,128)(2,1)S(1)}, u32[]{:S(2)}, u32[]{:S(2)}) collective-permute-start(bf16[128,4,128]{2,1,0:T(4,128)(2,1)S(1)} %pad_maximum_fusion.11), channel_id=1, source_target_pairs={{32,0},{64,32},{96,64},{128,96},{160,128},{192,160},{224,192},{256... | collective-permute-start | bytes 393224 | tf_op jit(solution)/shard_map/ppermute | solution.py:10
  56.3 8.1 %collective-permute-start.9 = (bf16[128,4,128]{2,1,0:T(4,128)(2,1)S(1)}, bf16[128,4,128]{2,1,0:T(4,128)(2,1)S(1)}, u32[]{:S(2)}, u32[]{:S(2)}) collective-permute-start(bf16[128,4,128]{2,1,0:T(4,128)(2,1)S(1)} %get-tuple-element.39), channel_id=1, source_target_pairs={{2,0},{4,2},{6,4},{8,6},{10,8},{12,10},{14,12},{16,14},{18,16},{20... | collective-permute-start | bytes 393224 | tf_op jit(solution)/shard_map/ppermute | solution.py:10
  58.2 6.2 %collective-permute-start.10 = (bf16[128,4,128]{2,1,0:T(4,128)(2,1)S(1)}, bf16[128,4,128]{2,1,0:T(4,128)(2,1)S(1)}, u32[]{:S(2)}, u32[]{:S(2)}) collective-permute-start(bf16[128,4,128]{2,1,0:T(4,128)(2,1)S(1)} %get-tuple-element.40), channel_id=1, source_target_pairs={{0,1},{2,3},{4,5},{6,7},{8,9},{10,11},{12,13},{14,15},{16,17},{18,... | collective-permute-start | bytes 393224 | tf_op jit(solution)/shard_map/ppermute | solution.py:10
  60.2 4.3 %collective-permute-start.11 = (bf16[128,4,128]{2,1,0:T(4,128)(2,1)S(1)}, bf16[128,4,128]{2,1,0:T(4,128)(2,1)S(1)}, u32[]{:S(2)}, u32[]{:S(2)}) collective-permute-start(bf16[128,4,128]{2,1,0:T(4,128)(2,1)S(1)} %get-tuple-element.37), channel_id=1, source_target_pairs={{1,0},{3,2},{5,4},{7,6},{9,8},{11,10},{13,12},{15,14},{17,16},{19,... | collective-permute-start | bytes 393224 | tf_op jit(solution)/shard_map/ppermute | solution.py:10
  67.3 0.9 copy-start.2
  70.0 19.0 %collective-permute-start.12 = (bf16[128,2,128]{2,1,0:T(2,128)(2,1)S(1)}, bf16[128,2,128]{2,1,0:T(2,128)(2,1)S(1)}, u32[]{:S(2)}, u32[]{:S(2)}) collective-permute-start(bf16[128,2,128]{2,1,0:T(2,128)(2,1)S(1)} %get-tuple-element.45), channel_id=1, source_target_pairs={{0,32},{32,64},{64,96},{96,128},{128,160},{160,192},{192,224},{224... | collective-permute-start | bytes 196616 | tf_op jit(solution)/shard_map/ppermute | solution.py:10
  72.3 0.8 copy-start.3
  74.4 15.9 %collective-permute-start.13 = (bf16[128,2,128]{2,1,0:T(2,128)(2,1)S(1)}, bf16[128,2,128]{2,1,0:T(2,128)(2,1)S(1)}, u32[]{:S(2)}, u32[]{:S(2)}) collective-permute-start(bf16[128,2,128]{2,1,0:T(2,128)(2,1)S(1)} %stack.190), channel_id=1, source_target_pairs={{32,0},{64,32},{96,64},{128,96},{160,128},{192,160},{224,192},{256... | collective-permute-start | bytes 196616 | tf_op jit(solution)/shard_map/ppermute | solution.py:10
  81.7 8.8 %collective-permute-start.14 = (bf16[128,2,128]{2,1,0:T(2,128)(2,1)S(1)}, bf16[128,2,128]{2,1,0:T(2,128)(2,1)S(1)}, u32[]{:S(2)}, u32[]{:S(2)}) collective-permute-start(bf16[128,2,128]{2,1,0:T(2,128)(2,1)S(1)} %get-tuple-element.42), channel_id=1, source_target_pairs={{0,2},{2,4},{4,6},{6,8},{8,10},{10,12},{12,14},{14,16},{16,18},{18... | collective-permute-start | bytes 196616 | tf_op jit(solution)/shard_map/ppermute | solution.py:10
  85.8 7.4 %collective-permute-start.15 = (bf16[128,2,128]{2,1,0:T(2,128)(2,1)S(1)}, bf16[128,2,128]{2,1,0:T(2,128)(2,1)S(1)}, u32[]{:S(2)}, u32[]{:S(2)}) collective-permute-start(bf16[128,2,128]{2,1,0:T(2,128)(2,1)S(1)} %get-tuple-element.43), channel_id=1, source_target_pairs={{2,0},{4,2},{6,4},{8,6},{10,8},{12,10},{14,12},{16,14},{18,16},{20... | collective-permute-start | bytes 196616 | tf_op jit(solution)/shard_map/ppermute | solution.py:10
  87.7 5.5 %collective-permute-start.16 = (bf16[128,2,128]{2,1,0:T(2,128)(2,1)S(1)}, bf16[128,2,128]{2,1,0:T(2,128)(2,1)S(1)}, u32[]{:S(2)}, u32[]{:S(2)}) collective-permute-start(bf16[128,2,128]{2,1,0:T(2,128)(2,1)S(1)} %get-tuple-element.44), channel_id=1, source_target_pairs={{0,1},{2,3},{4,5},{6,7},{8,9},{10,11},{12,13},{14,15},{16,17},{18,... | collective-permute-start | bytes 196616 | tf_op jit(solution)/shard_map/ppermute | solution.py:10
  89.0 4.3 %collective-permute-start.17 = (bf16[128,2,128]{2,1,0:T(2,128)(2,1)S(1)}, bf16[128,2,128]{2,1,0:T(2,128)(2,1)S(1)}, u32[]{:S(2)}, u32[]{:S(2)}) collective-permute-start(bf16[128,2,128]{2,1,0:T(2,128)(2,1)S(1)} %get-tuple-element.41), channel_id=1, source_target_pairs={{1,0},{3,2},{5,4},{7,6},{9,8},{11,10},{13,12},{15,14},{17,16},{19,... | collective-permute-start | bytes 196616 | tf_op jit(solution)/shard_map/ppermute | solution.py:10
  94.0 1.0 copy-start.1
where the time goes:
time: 97 us; the launch traced here: 96.2 us
  starting transfers between devices  62.5 us (64%)
  local copies, waits for them, and re-layouts  13.5 us (14%)
  other arithmetic  7.53 us (8%)
  waiting for transfers between devices  7.32 us (8%)
  matrix products  3.25 us (3%)
  between operations  2.08 us (2%)
    ppermute x18, starting transfers between devices, from_behind(): return lax.ppermute(x, axis, pairs)  55.9 us
    ppermute x18, waiting for transfers between devices, from_behind(): return lax.ppermute(x, axis, pairs)  6.65 us
    unnamed x35, local copies, waits for them, and re-layouts  5.51 us
    all_to_all x1, starting transfers between devices, body(): lax.all_to_all(outgoing, 'gz', split_axis=0, concat_axis=0, tiled=True)  3.44 us
    all_to_all x1, starting transfers between devices, body(): lax.all_to_all(label_out, 'gz', split_axis=0, concat_axis=0, tiled=True)  3.19 us
    slice x3, local copies, waits for them, and re-layouts, block_product(): halo[:, :, 1, :]  2.81 us
    another operation x5, other arithmetic, packed(): jnp.stack([matrix[:, which_block, :] for matrix in matrices for which_blo...  2.47 us
  transfers between devices with their start and end apart: 20, of which 5 were waited for; matrix products, arithmetic and copies ran while one was open for 9% of the time, Pallas kernels for 0%

commit v1 on v0

v1 whole, which is shorter than its diff:
```python
import jax
import jax.numpy as jnp
from jax import lax
from jax.experimental import pallas as pl
from jax.experimental.pallas import tpu as pltpu
from jax.sharding import PartitionSpec as P

MESH = pl.DeviceIdType.MESH
BLOCK = 128
SIDES = (1, 2, 3, 4, 5)
FACING = {1: 2, 2: 1, 3: 4, 4: 3, 5: 5}
FACE, OWN, NEXT, MIDDLE = range(4)


def dot(a, b):
    return jnp.dot(a, b, preferred_element_type=jnp.float32)


def kernel(
    sizes, s_hbm, columns_hbm, home_hbm, z_hbm, y_hbm, z_out, y_out,
    raw, columns, home, z_keep, y_keep, face_out, own_out, next_out, middle_out,
    face_in, own_in, next_in, middle_in, local_sem, move_send, move_recv, send, recv,
):
    n_x, n_y = sizes
    gx, gy, gz = lax.axis_index("gx"), lax.axis_index("gy"), lax.axis_index("gz")
    place = {1: (gx - 1, gy, gz), 2: (gx + 1, gy, gz), 3: (gx, gy - 1, gz), 4: (gx, gy + 1, gz), 5: (gx, gy, 1 - gz)}
    inside = {1: gx > 0, 2: gx < n_x - 1, 3: gy > 0, 4: gy < n_y - 1}
    slot = {1: 1, 2: 2, 3: 3, 4: 4, 5: 6 - gz}

    loads = [
        pltpu.make_async_copy(source, target, local_sem.at[i])
        for i, (source, target) in enumerate((
            (s_hbm, raw.at[0]), (columns_hbm, columns.at[0]), (home_hbm, home),
            (z_hbm, z_keep.at[0]), (y_hbm, y_keep),
        ))
    ]
    for load in loads:
        load.start()

    def on_side(c, run):
        if c in inside:
            pl.when(inside[c])(run)
        else:
            run()

    barrier = pltpu.get_barrier_semaphore()
    for c in SIDES:
        on_side(c, lambda c=c: pl.semaphore_signal(barrier, inc=1, device_id=place[c], device_id_type=MESH))
    count = 1 + sum(jnp.where(inside[c], 1, 0) for c in inside)
    pl.semaphore_wait(barrier, count)

    def remote(source, target, s_sem, r_sem, c):
        return pltpu.make_async_remote_copy(
            src_ref=source, dst_ref=target, send_sem=s_sem, recv_sem=r_sem, device_id=place[c], device_id_type=MESH
        )

    moves = [
        remote(columns_hbm, columns.at[1], move_send.at[0], move_recv.at[0], 5),
        remote(s_hbm, raw.at[1], move_send.at[1], move_recv.at[1], 5),
    ]
    for move in moves:
        move.start()
    keeps = {c: remote(z_hbm, z_keep.at[FACING[c]], send.at[4, c], recv.at[4, FACING[c]], c) for c in SIDES}
    def arrival(buffer, message, c):
        return pltpu.make_async_remote_copy(
            src_ref=buffer.at[c], dst_ref=buffer.at[c], send_sem=send.at[message, c], recv_sem=recv.at[message, c],
            device_id=place[c], device_id_type=MESH,
        )

    for c in SIDES:
        on_side(c, keeps[c].start)

    for load in loads[1:]:
        load.wait()
    loads[0].wait()
    for move in moves:
        move.wait()

    stay = home[0] == gz
    block = [jnp.where(stay, raw[0, k], raw[1, k]) for k in range(4)]
    column = [jnp.where(stay, columns[0, 0, k], columns[1, 0, k]) for k in range(4)]
    zero = jnp.zeros((BLOCK, BLOCK), jnp.bfloat16)
    square, keep_y, keep_z = {0: block[0]}, {}, {}
    for c in SIDES:
        valid = inside.get(c, True)
        found = zero
        for k in (1, 2, 3):
            found = jnp.where(jnp.logical_and(column[k] == slot[c], valid), block[k], found)
        square[c] = found
        keep_y[c] = jnp.logical_and(y_keep[0, slot[c]] == 1, valid)
        keep_z[c] = jnp.logical_and(z_keep[0, 0, slot[c]] == 1, valid)

    own_out[...] = square[0]
    face = {}
    for c in SIDES:
        face[c] = jnp.where(keep_y[c], square[c], zero)
        face_out[c] = face[c]
        if c in inside:
            @pl.when(jnp.logical_not(inside[c]))
            def _():
                for buffer in (face_in, own_in, next_in, middle_in):
                    buffer[c] = zero

    def send_to(source, target, message, c):
        return remote(source, target.at[FACING[c]], send.at[message, c], recv.at[message, FACING[c]], c)

    faces = {c: send_to(face_out.at[c], face_in, FACE, c) for c in SIDES}
    owns = {c: send_to(own_out, own_in, OWN, c) for c in SIDES}
    for c in SIDES:
        on_side(c, faces[c].start)
    for c in SIDES:
        on_side(c, owns[c].start)

    row = lax.broadcasted_iota(jnp.int32, (BLOCK, BLOCK), 0)
    lane = lax.broadcasted_iota(jnp.int32, (BLOCK, BLOCK), 1)
    lifted = jnp.where(row == lane, 1.5, 0.0).astype(jnp.float32)

    def half(x):
        return (x.astype(jnp.float32) * -0.5).astype(jnp.bfloat16)

    def centre(x):
        return (lifted - 0.5 * x.astype(jnp.float32)).astype(jnp.bfloat16)

    def kept(mask, x):
        return jnp.where(mask, x, jnp.zeros_like(x))

    middle = {0: centre(square[0])}
    inverse = {0: middle[0]}
    for c in SIDES:
        middle[c] = half(face[c])
        inverse[c] = kept(keep_z[c], middle[c])
    first = {c: dot(square[0], middle[c]) for c in (0,) + SIDES}

    for c in SIDES:
        on_side(c, arrival(face_in, FACE, c).wait_recv)
        on_side(c, arrival(z_keep, 4, c).wait_recv)
    near_face = {c: face_in[c] for c in SIDES}
    total = first[0]
    for c in SIDES:
        total = total - 0.5 * dot(square[c], near_face[c])
    square_next = {0: total.astype(jnp.bfloat16)}
    next_out[...] = square_next[0]
    nexts = {c: send_to(next_out, next_in, NEXT, c) for c in SIDES}
    for c in SIDES:
        on_side(c, nexts[c].start)

    near_middle = {c: half(near_face[c]) for c in SIDES}
    facing_slot = {1: 2, 2: 1, 3: 4, 4: 3, 5: 5 + gz}
    near_inverse = {}
    for c in SIDES:
        flag = jnp.logical_and(z_keep[c, 0, facing_slot[c]] == 1, inside.get(c, True))
        near_inverse[c] = kept(flag, near_middle[c])
    part_near_next = {c: dot(near_face[c], middle[0]) for c in SIDES}
    part_near_quad = {c: dot(near_inverse[c], square_next[0]) for c in SIDES}

    for c in SIDES:
        on_side(c, arrival(own_in, OWN, c).wait_recv)
    near_own = {c: own_in[c] for c in SIDES}
    near_centre = {c: centre(near_own[c]) for c in SIDES}
    near_next = {}
    for c in SIDES:
        near_next[c] = (part_near_next[c] + dot(near_own[c], near_middle[c])).astype(jnp.bfloat16)
    quad = dot(inverse[0], square_next[0])
    for c in SIDES:
        quad = quad + dot(inverse[c], near_next[c])
    last = {0: (lifted - 0.5 * quad).astype(jnp.bfloat16)}
    middle_out[...] = last[0]
    middles = {c: send_to(middle_out, middle_in, MIDDLE, c) for c in SIDES}
    for c in SIDES:
        on_side(c, middles[c].start)

    for c in SIDES:
        square_next[c] = kept(keep_y[c], first[c] + dot(square[c], near_centre[c])).astype(jnp.bfloat16)
    part_quad = {c: dot(inverse[0], square_next[c]) for c in SIDES}
    y_total = dot(square_next[0], last[0])
    for c in SIDES:
        near_last = (-0.5 * (part_near_quad[c] + dot(near_centre[c], near_next[c]))).astype(jnp.bfloat16)
        y_total = y_total + dot(square_next[c], near_last)
    y_out[0] = y_total.astype(jnp.bfloat16)

    z_total = dot(last[0], inverse[0])
    z_part = {c: dot(last[0], inverse[c]) for c in SIDES}
    for c in SIDES:
        on_side(c, arrival(next_in, NEXT, c).wait_recv)
    for c in SIDES:
        whole = part_quad[c] + dot(inverse[c], next_in[c])
        last[c] = kept(keep_y[c], -0.5 * whole).astype(jnp.bfloat16)
        z_total = z_total + dot(last[c], near_inverse[c])
        z_part[c] = z_part[c] + dot(last[c], near_centre[c])
    z_out[0] = z_total.astype(jnp.bfloat16)
    for c in SIDES:
        z_out[slot[c]] = kept(keep_z[c], z_part[c]).astype(jnp.bfloat16)
    z_out[facing_slot[5]] = zero
    y_out[facing_slot[5]] = zero
    y_part = {c: dot(square_next[0], last[c]) for c in SIDES}
    for c in SIDES:
        on_side(c, arrival(middle_in, MIDDLE, c).wait_recv)
    for c in SIDES:
        y_out[slot[c]] = kept(keep_y[c], y_part[c] + dot(square_next[c], middle_in[c])).astype(jnp.bfloat16)
    for group in (keeps, faces, owns, nexts, middles):
        for c in SIDES:
            on_side(c, group[c].wait_send)


def solution(mesh):
    sizes = (mesh.shape["gx"], mesh.shape["gy"])

    def step(s_blocks, s_columns, new_home, z_pattern, y_pattern):
        any_spec = pl.BlockSpec(memory_space=pl.ANY)
        vmem = pl.BlockSpec(memory_space=pltpu.VMEM)
        blocks = jax.ShapeDtypeStruct((7, BLOCK, BLOCK), jnp.bfloat16)
        buffer = pltpu.VMEM((6, BLOCK, BLOCK), jnp.bfloat16)
        single = pltpu.VMEM((BLOCK, BLOCK), jnp.bfloat16)
        dma = pltpu.SemaphoreType.DMA
        z, y = pl.pallas_call(
            lambda *refs: kernel(sizes, *refs),
            name="newton_schulz",
            out_shape=(blocks, blocks),
            in_specs=[any_spec] * 5,
            out_specs=(vmem, vmem),
            scratch_shapes=[
                pltpu.VMEM((2, 4, BLOCK, BLOCK), jnp.bfloat16),
                pltpu.SMEM((2, 1, 4), jnp.int32),
                pltpu.SMEM((1,), jnp.int32),
                pltpu.SMEM((6, 1, 7), jnp.int32),
                pltpu.SMEM((1, 7), jnp.int32),
                buffer, single, single, single,
                buffer, buffer, buffer, buffer,
                dma((5,)), dma((2,)), dma((2,)), dma((5, 6)), dma((5, 6)),
            ],
            compiler_params=pltpu.CompilerParams(collective_id=0, has_side_effects=True),
        )(s_blocks[0], s_columns, new_home, z_pattern, y_pattern)
        return jnp.transpose(z, (1, 0, 2))[None], jnp.transpose(y, (1, 0, 2))[None]

    row = P(("gx", "gy", "gz"))
    wide = P(("gx", "gy", "gz"), None)
    block = P(("gx", "gy", "gz"), None, None, None)
    return jax.shard_map(
        step, mesh=mesh, in_specs=(block, wide, row, wide, wide), out_specs=(block, block), check_vma=False
    )
```

time: 97 us -> 28.2 us (0.29)
  the two profiles are of different devices: /device:TPU:480 before, /device:TPU:1 now
where the time goes in v1:
time: 28.2 us; the launch traced here: 27.9 us
  Pallas kernels  24.2 us (86%)
  local copies, waits for them, and re-layouts  2.37 us (8%)
  between operations  1.29 us (5%)
    pallas_call x1, Pallas kernels, step(): pl.pallas_call(lambda *refs: kernel(sizes, *refs), name='newton_schulz',...  24.2 us
    unnamed x4, local copies, waits for them, and re-layouts  2.37 us

profile of v1, /device:TPU:1, one launch (start us, length us, event | category | flops | bytes accessed | tf_op | source)
XLA Modules:
  0.0 27.9 jit_solution(515151338207527939)
XLA Ops:
  1.3 24.2 %newton_schulz.1 = (bf16[7,128,128]{2,1,0:T(8,128)(2,1)}, bf16[7,128,128]{2,1,0:T(8,128)(2,1)}) custom-call(bf16[4,128,128]{2,1,0:T(8,128)(2,1)} %bitcast.9, s32[1,4]{1,0:T(1,128)} %refs_1_.1, s32[1]{0:T(128)S(6)} %copy.9.refs_2_, s32[1,7]{1,0:T(1,128)} %refs_3_.1, s32[1,7]{1,0:T(1,128)} %refs_4_.1), custom_call_target="tpu_custom_call" | custom-call | tf_op jit(solution)/shard_map/newton_schulz/pallas_call | solution.py:215
  25.5 0.0 copy-start
  25.5 1.7 %copy.10 = bf16[1,128,7,128]{3,1,2,0:T(8,128)(2,1)} copy(bf16[1,128,7,128]{3,1,2,0:T(8,128)(2,1)} %bitcast.8) | data formatting | bytes 458752
  27.2 0.0 copy-done
  27.2 0.7 %copy.11 = bf16[1,128,7,128]{3,1,2,0:T(8,128)(2,1)} copy(bf16[1,128,7,128]{3,1,2,0:T(8,128)(2,1)S(1)} %bitcast.7) | data formatting | bytes 458752
Async XLA Ops:
  25.5 1.7 %copy-start = (bf16[7,128,128]{2,1,0:T(8,128)(2,1)S(1)}, bf16[7,128,128]{2,1,0:T(8,128)(2,1)}, u32[]{:S(2)}) copy-start(bf16[7,128,128]{2,1,0:T(8,128)(2,1)} %get-tuple-element.5) | copy-start | bytes 688132

commit v2 on v1

v2 whole, which is shorter than its diff:
```python
import jax
import jax.numpy as jnp
from jax import lax
from jax.experimental import pallas as pl
from jax.experimental.pallas import tpu as pltpu
from jax.sharding import PartitionSpec as P

MESH = pl.DeviceIdType.MESH
BLOCK = 128
LINKS = (1, 2, 3, 4)
SIDES = LINKS + (5,)
FACING = {1: 2, 2: 1, 3: 4, 4: 3, 5: 5}


def dot(a, b):
    return jnp.dot(a, b, preferred_element_type=jnp.float32)


def beside(parts):
    return jnp.concatenate(parts, axis=1)


def below(parts):
    return jnp.concatenate(parts, axis=0)


def kernel(
    sizes, s_hbm, columns_hbm, home_hbm, z_hbm, y_hbm, z_out, y_out,
    raw, columns, home, z_keep, y_keep, face_out, own_out, next_out, middle_out,
    face_in, own_in, next_in, middle_in, local_sem, pair_sem, move, row_send, row_recv,
    send, face_recv, own_recv, next_recv, middle_recv,
):
    n_x, n_y = sizes
    gx, gy, gz = lax.axis_index("gx"), lax.axis_index("gy"), lax.axis_index("gz")
    place = {1: (gx - 1, gy, gz), 2: (gx + 1, gy, gz), 3: (gx, gy - 1, gz), 4: (gx, gy + 1, gz), 5: (gx, gy, 1 - gz)}
    inside = {1: gx > 0, 2: gx < n_x - 1, 3: gy > 0, 4: gy < n_y - 1}
    slot = {1: 1, 2: 2, 3: 3, 4: 4, 5: 6 - gz}
    facing_slot = {1: 2, 2: 1, 3: 4, 4: 3, 5: 5 + gz}

    loads = [
        pltpu.make_async_copy(source, target, local_sem.at[i])
        for i, (source, target) in enumerate((
            (s_hbm, raw.at[pl.ds(0, 4)]), (columns_hbm, columns.at[0]), (home_hbm, home),
            (z_hbm, z_keep.at[0]), (y_hbm, y_keep),
        ))
    ]

    def on_side(c, run):
        if c in inside:
            pl.when(inside[c])(run)
        else:
            run()

    for load in loads:
        load.start()
    low, high = gz == 0, gz == 1
    barrier = pltpu.get_barrier_semaphore()

    def signal(semaphore, device):
        pl.semaphore_signal(semaphore, inc=1, device_id=device, device_id_type=MESH)

    @pl.when(high)
    def _():
        signal(barrier, place[5])

    @pl.when(low)
    def _():
        pl.semaphore_wait(barrier, 1)
        signal(pair_sem, place[5])

    @pl.when(high)
    def _():
        pl.semaphore_wait(pair_sem, 1)
        for c in LINKS:
            @pl.when(inside[c])
            def _():
                signal(barrier, place[c])

    def remote(source, target, s_sem, r_sem, device):
        return pltpu.make_async_remote_copy(
            src_ref=source, dst_ref=target, send_sem=s_sem, recv_sem=r_sem, device_id=device, device_id_type=MESH
        )

    moves = [
        remote(columns_hbm, columns.at[1], move.at[0], move.at[1], place[5]),
        remote(s_hbm, raw.at[pl.ds(4, 4)], move.at[2], move.at[3], place[5]),
    ]
    moves[0].start()

    @pl.when(low)
    def _():
        moves[1].start()

    loads[0].wait()

    @pl.when(high)
    def _():
        remote(raw.at[pl.ds(0, 4)], raw.at[pl.ds(4, 4)], move.at[2], move.at[3], place[5]).start()
        pl.semaphore_wait(barrier, sum(jnp.where(inside[c], 1, 0) for c in LINKS))
        signal(pair_sem, place[5])

    @pl.when(low)
    def _():
        pl.semaphore_wait(pair_sem, 1)

    def row_copy(c, end):
        return remote(z_hbm, z_keep.at[end], row_send.at[c], row_recv.at[end], place[c])

    for c in SIDES:
        on_side(c, row_copy(c, FACING[c]).start)

    def send_to(source, target, sems):
        for c in SIDES:
            part = source.at[c] if len(source.shape) == 3 else source
            on_side(c, remote(part, target.at[FACING[c]], send.at[c], sems.at[FACING[c]], place[c]).start)

    def arrived(buffer, sems, c):
        on_side(c, remote(buffer.at[c], buffer.at[c], send.at[c], sems.at[c], place[c]).wait_recv)

    zero = jnp.zeros((BLOCK, BLOCK), jnp.bfloat16)
    raw[8] = zero
    for c in LINKS:
        @pl.when(jnp.logical_not(inside[c]))
        def _():
            for buffer in (face_in, own_in, next_in, middle_in):
                buffer[c] = zero
            for i in range(7):
                z_keep[c, 0, i] = 0
    for load in loads[1:]:
        load.wait()
    moves[0].wait_recv()
    stay = home[0, 0] == gz
    base = jnp.where(stay, 0, 4)
    column = [jnp.where(stay, columns[0, 0, k], columns[1, 0, k]) for k in range(4)]
    found, kept_found, keep_y, keep_z = {}, {}, {}, {}
    for c in SIDES:
        valid = inside.get(c, True)
        index = jnp.int32(8)
        for k in (1, 2, 3):
            index = jnp.where(column[k] == slot[c], base + k, index)
        keep_y[c] = jnp.logical_and(y_keep[0, slot[c]] == 1, valid)
        keep_z[c] = jnp.logical_and(z_keep[0, 0, slot[c]] == 1, valid)
        found[c] = jnp.where(valid, index, 8)
        kept_found[c] = jnp.where(keep_y[c], index, 8)
    moves[1].wait_recv()

    face = {}
    for c in SIDES:
        face[c] = raw[kept_found[c]]
        face_out[c] = face[c]
    square = {0: raw[base]}
    own_out[...] = square[0]
    send_to(face_out, face_in, face_recv)
    for c in LINKS:
        on_side(c, remote(own_out, own_in.at[FACING[c]], send.at[c], own_recv.at[FACING[c]], place[c]).start)

    row = lax.broadcasted_iota(jnp.int32, (BLOCK, BLOCK), 0)
    lane = lax.broadcasted_iota(jnp.int32, (BLOCK, BLOCK), 1)
    lifted = jnp.where(row == lane, 1.5, 0.0).astype(jnp.float32)

    def half(x):
        return (x.astype(jnp.float32) * -0.5).astype(jnp.bfloat16)

    def centre(x):
        return (lifted - 0.5 * x.astype(jnp.float32)).astype(jnp.bfloat16)

    def kept(mask, x):
        return jnp.where(mask, x, jnp.zeros_like(x))

    moves[0].wait_send()

    middle = {0: centre(square[0])}
    inverse = {0: middle[0]}
    for c in SIDES:
        square[c] = raw[found[c]]
        middle[c] = half(face[c])
        inverse[c] = kept(keep_z[c], middle[c])
    first = {c: dot(square[0], middle[c]) for c in (0,) + SIDES}
    near_flag = {}
    for c in SIDES:
        on_side(c, row_copy(c, c).wait_recv)
        near_flag[c] = jnp.logical_and(z_keep[c, 0, facing_slot[c]] == 1, inside.get(c, True))

    for c in SIDES:
        arrived(face_in, face_recv, c)
    near_face = {c: face_in[c] for c in SIDES}
    total = first[0] - 0.5 * dot(beside([square[c] for c in SIDES]), below([near_face[c] for c in SIDES]))
    square_next = {0: total.astype(jnp.bfloat16)}
    next_out[...] = square_next[0]
    send_to(next_out, next_in, next_recv)

    spread = dot(below([near_face[c] for c in SIDES]), middle[0])
    for c in LINKS:
        arrived(own_in, own_recv, c)
    near_own, near_next = {}, {}
    for i, c in enumerate(SIDES):
        near_own[c] = raw[4 - base] if c == 5 else own_in[c]
        part = spread[i * BLOCK:(i + 1) * BLOCK]
        near_next[c] = (part - 0.5 * dot(near_own[c], near_face[c])).astype(jnp.bfloat16)
    quad = dot(
        beside([inverse[c] for c in (0,) + SIDES]), below([square_next[0]] + [near_next[c] for c in SIDES])
    )
    last = {0: (lifted - 0.5 * quad).astype(jnp.bfloat16)}
    middle_out[...] = last[0]
    send_to(middle_out, middle_in, middle_recv)
    moves[1].wait_send()

    near_centre, near_inverse, near_last, part_quad = {}, {}, {}, {}
    for c in SIDES:
        near_centre[c] = centre(near_own[c])
        square_next[c] = kept(keep_y[c], first[c] + dot(square[c], near_centre[c])).astype(jnp.bfloat16)
        near_inverse[c] = kept(near_flag[c], half(near_face[c]))
        part_quad[c] = dot(inverse[0], square_next[c])
        near_quad = dot(beside([near_inverse[c], near_centre[c]]), below([square_next[0], near_next[c]]))
        near_last[c] = (-0.5 * near_quad).astype(jnp.bfloat16)
    y_total = dot(
        beside([square_next[c] for c in (0,) + SIDES]), below([last[0]] + [near_last[c] for c in SIDES])
    )
    y_out[0] = y_total.astype(jnp.bfloat16)
    z_out[facing_slot[5]] = zero
    y_out[facing_slot[5]] = zero

    for c in SIDES:
        arrived(next_in, next_recv, c)
    y_part = {}
    for c in SIDES:
        last[c] = kept(keep_y[c], -0.5 * (part_quad[c] + dot(inverse[c], next_in[c]))).astype(jnp.bfloat16)
        z_part = dot(beside([last[0], last[c]]), below([inverse[c], near_centre[c]]))
        z_out[slot[c]] = kept(keep_z[c], z_part).astype(jnp.bfloat16)
        y_part[c] = dot(square_next[0], last[c])
    z_total = dot(
        beside([last[c] for c in (0,) + SIDES]), below([inverse[0]] + [near_inverse[c] for c in SIDES])
    )
    z_out[0] = z_total.astype(jnp.bfloat16)

    for c in SIDES:
        arrived(middle_in, middle_recv, c)
    for c in SIDES:
        y_out[slot[c]] = kept(keep_y[c], y_part[c] + dot(square_next[c], middle_in[c])).astype(jnp.bfloat16)

    def drained(c, blocks):
        part = raw.at[pl.ds(0, blocks)]
        remote(part, part, send.at[c], face_recv.at[c], place[c]).wait_send()
        row_copy(c, c).wait_send()

    drained(5, 3)
    for c in LINKS:
        @pl.when(inside[c])
        def _():
            drained(c, 4)


def store(z_in, y_in, z_out, y_out, sem):
    copies = [pltpu.make_async_copy(z_in, z_out, sem.at[0]), pltpu.make_async_copy(y_in, y_out, sem.at[1])]
    for copy in copies:
        copy.start()
    for copy in copies:
        copy.wait()


def solution(mesh):
    sizes = (mesh.shape["gx"], mesh.shape["gy"])

    def step(s_blocks, s_columns, new_home, z_pattern, y_pattern):
        any_spec = pl.BlockSpec(memory_space=pl.ANY)
        vmem = pl.BlockSpec(memory_space=pltpu.VMEM)
        buffer = pltpu.VMEM((6, BLOCK, BLOCK), jnp.bfloat16)
        single = pltpu.VMEM((BLOCK, BLOCK), jnp.bfloat16)
        dma = pltpu.SemaphoreType.DMA
        z, y = pl.pallas_call(
            lambda *refs: kernel(sizes, *refs),
            name="newton_schulz",
            out_shape=(pltpu.VMEM((7, BLOCK, BLOCK), jnp.bfloat16),) * 2,
            in_specs=[any_spec] * 5,
            out_specs=(vmem, vmem),
            scratch_shapes=[
                pltpu.VMEM((9, BLOCK, BLOCK), jnp.bfloat16),
                pltpu.SMEM((2, 1, 4), jnp.int32),
                pltpu.SMEM((1, 1), jnp.int32),
                pltpu.SMEM((6, 1, 7), jnp.int32),
                pltpu.SMEM((1, 7), jnp.int32),
                buffer, single, single, single,
                buffer, buffer, buffer, buffer,
                dma((5,)), pltpu.SemaphoreType.REGULAR, dma((4,)), dma((6,)), dma((6,)),
                dma((6,)), dma((6,)), dma((6,)), dma((6,)), dma((6,)),
            ],
            compiler_params=pltpu.CompilerParams(collective_id=0, has_side_effects=True),
        )(s_blocks[0], s_columns, new_home.reshape(1, 1), z_pattern, y_pattern)
        z, y = pl.pallas_call(
            store,
            name="store",
            out_shape=(jax.ShapeDtypeStruct((7, BLOCK, BLOCK), jnp.bfloat16),) * 2,
            in_specs=[any_spec] * 2,
            out_specs=(any_spec,) * 2,
            scratch_shapes=[dma((2,))],
            compiler_params=pltpu.CompilerParams(vmem_limit_bytes=1 << 20),
        )(z, y)
        return jnp.transpose(z, (1, 0, 2))[None], jnp.transpose(y, (1, 0, 2))[None]

    row = P(("gx", "gy", "gz"))
    wide = P(("gx", "gy", "gz"), None)
    block = P(("gx", "gy", "gz"), None, None, None)
    return jax.shard_map(
        step, mesh=mesh, in_specs=(block, wide, row, wide, wide), out_specs=(block, block), check_vma=False
    )
```

time: 28.2 us -> 24.2 us (0.86)
  local copies, waits for them, and re-layouts: 2.37 us -> 0 us
  Pallas kernels: 24.2 us -> 22.8 us
    unnamed x4 -> x0, local copies, waits for them, and re-layouts: 2.37 us -> none
    pallas_call x1, Pallas kernels: 24.2 us -> 22 us  [step(): pl.pallas_call(lambda *refs: kernel(sizes, *refs), name='newton_schulz',...]
    pallas_call x0 -> x1, Pallas kernels: none -> 0.78 us  [step(): pl.pallas_call(store, name='store', out_shape=(jax.ShapeDtypeStruct((7, B...]
where the time goes in v2:
time: 24.2 us; the launch traced here: 24 us
  Pallas kernels  22.8 us (94%)
  between operations  1.28 us (5%)
    pallas_call x1, Pallas kernels, step(): pl.pallas_call(lambda *refs: kernel(sizes, *refs), name='newton_schulz',...  22 us
    pallas_call x1, Pallas kernels, step(): pl.pallas_call(store, name='store', out_shape=(jax.ShapeDtypeStruct((7, B...  0.78 us

profile of v2, /device:TPU:1, one launch (start us, length us, event | category | flops | bytes accessed | tf_op | source)
XLA Modules:
  0.0 24.0 jit_solution(6596858243446112732)
XLA Ops:
  1.3 22.0 %newton_schulz.1 = (bf16[7,128,128]{2,1,0:T(8,128)(2,1)S(1)}, bf16[7,128,128]{2,1,0:T(8,128)(2,1)S(1)}) custom-call(bf16[4,128,128]{2,1,0:T(8,128)(2,1)} %bitcast.9, s32[1,4]{1,0:T(1,128)} %refs_1_.1, s32[1,1]{1,0:T(1,128)} %bitcast.8.refs_2_, s32[1,7]{1,0:T(1,128)} %refs_3_.1, s32[1,7]{1,0:T(1,128)} %refs_4_.1), custom_call_target="tpu_custom_call" | custom-call | tf_op jit(solution)/shard_map/newton_schulz/pallas_call | solution.py:270
  23.3 0.8 %store.1 = (bf16[7,128,128]{2,1,0:T(8,128)(2,1)}, bf16[7,128,128]{2,1,0:T(8,128)(2,1)}) custom-call(bf16[7,128,128]{2,1,0:T(8,128)(2,1)S(1)} %get-tuple-element.6.z_in, bf16[7,128,128]{2,1,0:T(8,128)(2,1)S(1)} %get-tuple-element.7.y_in), custom_call_target="tpu_custom_call" | custom-call | tf_op jit(solution)/shard_map/store/pallas_call | solution.py:289

commit v3 on v2

v3 whole, which is shorter than its diff:
```python
import functools

import jax
import jax.numpy as jnp
from jax import lax
from jax.experimental import pallas as pl
from jax.experimental.pallas import tpu as pltpu
from jax.sharding import PartitionSpec as P

MESH = pl.DeviceIdType.MESH
BLOCK = 128
LINKS = (1, 2, 3, 4)
SIDES = LINKS + (5,)
FACING = {1: 2, 2: 1, 3: 4, 4: 3, 5: 5}


def dot(a, b):
    return jnp.dot(a, b, preferred_element_type=jnp.float32)


def beside(parts):
    return jnp.concatenate(parts, axis=1)


def below(parts):
    return jnp.concatenate(parts, axis=0)


def at_once(lefts, rights):
    return dot(beside(lefts), below(rights))


def each(lefts, rights):
    return functools.reduce(jnp.add, [dot(left, right) for left, right in zip(lefts, rights)])


def kernel(
    sizes, s_hbm, columns_hbm, home_hbm, z_hbm, y_hbm, z_out, y_out,
    raw, columns, home, z_keep, y_keep, face_out, own_out, next_out, middle_out,
    face_in, own_in, next_in, middle_in, local_sem, pair_sem, move, z_send, z_recv, y_sem,
    send, face_recv, own_recv, next_recv, middle_recv,
):
    n_x, n_y = sizes
    gx, gy, gz = lax.axis_index("gx"), lax.axis_index("gy"), lax.axis_index("gz")
    place = {1: (gx - 1, gy, gz), 2: (gx + 1, gy, gz), 3: (gx, gy - 1, gz), 4: (gx, gy + 1, gz), 5: (gx, gy, 1 - gz)}
    inside = {1: gx > 0, 2: gx < n_x - 1, 3: gy > 0, 4: gy < n_y - 1}
    slot = {1: 1, 2: 2, 3: 3, 4: 4, 5: 6 - gz}
    facing_slot = {1: 2, 2: 1, 3: 4, 4: 3, 5: 5 + gz}
    low, high = gz == 0, gz == 1

    loads = [
        pltpu.make_async_copy(source, target, local_sem.at[i])
        for i, (source, target) in enumerate((
            (s_hbm, raw.at[pl.ds(0, 4)]), (columns_hbm, columns.at[0]), (home_hbm, home),
            (z_hbm, z_keep.at[0]), (y_hbm, y_keep.at[0]),
        ))
    ]

    def on_side(c, run):
        if c in inside:
            pl.when(inside[c])(run)
        else:
            run()

    def remote(source, target, s_sem, r_sem, device):
        return pltpu.make_async_remote_copy(
            src_ref=source, dst_ref=target, send_sem=s_sem, recv_sem=r_sem, device_id=device, device_id_type=MESH
        )

    for load in loads:
        load.start()
    barrier = pltpu.get_barrier_semaphore()

    def signal(semaphore, device):
        pl.semaphore_signal(semaphore, inc=1, device_id=device, device_id_type=MESH)

    @pl.when(high)
    def _():
        signal(barrier, place[5])

    moves = [
        remote(columns_hbm, columns.at[1], move.at[0], move.at[1], place[5]),
        remote(s_hbm, raw.at[pl.ds(4, 4)], move.at[2], move.at[3], place[5]),
    ]

    @pl.when(low)
    def _():
        pl.semaphore_wait(barrier, 1)
        signal(pair_sem, place[5])
        moves[1].start()
        moves[0].start()

    for c in LINKS:
        @pl.when(inside[c])
        def _():
            x, y, _ = place[c]
            signal(barrier, (x, y, 1))

    zero = jnp.zeros((BLOCK, BLOCK), jnp.bfloat16)
    raw[8] = zero

    loads[0].wait()

    @pl.when(high)
    def _():
        pl.semaphore_wait(pair_sem, 1)
        remote(raw.at[pl.ds(0, 4)], raw.at[pl.ds(4, 4)], move.at[2], move.at[3], place[5]).start()
        moves[0].start()
        pl.semaphore_wait(barrier, sum(jnp.where(inside[c], 2, 0) for c in LINKS))
        signal(pair_sem, place[5])

    for load in loads[1:]:
        load.wait()

    def z_copy(c, end):
        return remote(z_hbm, z_keep.at[end], z_send.at[c - 1], z_recv.at[end - 1], place[c])

    y_copy = remote(y_hbm, y_keep.at[1], y_sem.at[0], y_sem.at[1], place[5])
    y_copy.start()
    z_copy(5, 5).start()
    moves[0].wait_recv()
    stay = home[0, 0] == gz
    base = jnp.where(stay, 0, 4)
    column = [jnp.where(stay, columns[0, 0, k], columns[1, 0, k]) for k in range(4)]
    other_column = [jnp.where(stay, columns[1, 0, k], columns[0, 0, k]) for k in range(4)]

    def pick(entries, wanted, first):
        index = jnp.int32(8)
        for k in (1, 2, 3):
            index = jnp.where(entries[k] == wanted, first + k, index)
        return index

    found, kept_found, keep_y, keep_z = {}, {}, {}, {}
    for c in SIDES:
        valid = inside.get(c, True)
        index = pick(column, slot[c], base)
        keep_y[c] = jnp.logical_and(y_keep[0, 0, slot[c]] == 1, valid)
        keep_z[c] = jnp.logical_and(z_keep[0, 0, slot[c]] == 1, valid)
        found[c] = jnp.where(valid, index, 8)
        kept_found[c] = jnp.where(keep_y[c], index, 8)

    moves[1].wait_recv()
    square = {0: raw[base]}
    own_out[...] = square[0]
    for c in LINKS:
        face_out[c] = raw[kept_found[c]]

    @pl.when(low)
    def _():
        pl.semaphore_wait(pair_sem, 1)

    for c in LINKS:
        on_side(c, remote(face_out.at[c], face_in.at[FACING[c]], send.at[c - 1], face_recv.at[FACING[c] - 1], place[c]).start)
    for c in LINKS:
        on_side(c, remote(own_out, own_in.at[FACING[c]], send.at[c - 1], own_recv.at[FACING[c] - 1], place[c]).start)
    for c in LINKS:
        on_side(c, z_copy(c, FACING[c]).start)
    moves[0].wait_send()

    for c in LINKS:
        @pl.when(jnp.logical_not(inside[c]))
        def _():
            for buffer in (face_in, own_in, next_in, middle_in):
                buffer[c] = zero
            for i in range(7):
                z_keep[c, 0, i] = 0

    def send_to(source, target, sems):
        for c in SIDES:
            on_side(c, remote(source, target.at[FACING[c]], send.at[c - 1], sems.at[FACING[c] - 1], place[c]).start)

    def arrived(buffer, sems, c):
        on_side(c, remote(buffer.at[c], buffer.at[c], send.at[c - 1], sems.at[c - 1], place[c]).wait_recv)

    row = lax.broadcasted_iota(jnp.int32, (BLOCK, BLOCK), 0)
    lane = lax.broadcasted_iota(jnp.int32, (BLOCK, BLOCK), 1)
    lifted = jnp.where(row == lane, 1.5, 0.0).astype(jnp.float32)

    def half(x):
        return (x.astype(jnp.float32) * -0.5).astype(jnp.bfloat16)

    def centre(x):
        return (lifted - 0.5 * x.astype(jnp.float32)).astype(jnp.bfloat16)

    def kept(mask, x):
        return jnp.where(mask, x, jnp.zeros_like(x))


    middle = {0: centre(square[0])}
    inverse = {0: middle[0]}
    for c in SIDES:
        square[c] = raw[found[c]]
        middle[c] = half(raw[kept_found[c]])
        inverse[c] = kept(keep_z[c], middle[c])
    first = {c: dot(square[0], middle[c]) for c in (0,) + SIDES}
    moves[1].wait_send()
    y_copy.wait_recv()
    near_index = pick(other_column, facing_slot[5], 4 - base)

    for c in LINKS:
        arrived(face_in, face_recv, c)
    near_face = {c: face_in[c] for c in LINKS}
    near_face[5] = raw[jnp.where(y_keep[1, 0, facing_slot[5]] == 1, near_index, 8)]
    total = first[0] - 0.5 * at_once([square[c] for c in SIDES], [near_face[c] for c in SIDES])
    square_next = {0: total.astype(jnp.bfloat16)}
    next_out[...] = square_next[0]
    send_to(next_out, next_in, next_recv)

    spread = dot(below([near_face[c] for c in SIDES]), middle[0])
    near_own, near_next = {5: raw[4 - base]}, {}
    for c in LINKS:
        arrived(own_in, own_recv, c)
    for i, c in enumerate(SIDES):
        if c in LINKS:
            near_own[c] = own_in[c]
        part = spread[i * BLOCK:(i + 1) * BLOCK]
        near_next[c] = (part - 0.5 * dot(near_own[c], near_face[c])).astype(jnp.bfloat16)
    quad = each([inverse[c] for c in (0,) + SIDES], [square_next[0]] + [near_next[c] for c in SIDES])
    last = {0: (lifted - 0.5 * quad).astype(jnp.bfloat16)}
    middle_out[...] = last[0]
    send_to(middle_out, middle_in, middle_recv)
    y_copy.wait_send()

    near_flag = {}
    for c in SIDES:
        on_side(c, z_copy(c, c).wait_recv)
        near_flag[c] = jnp.logical_and(z_keep[c, 0, facing_slot[c]] == 1, inside.get(c, True))
    near_centre, near_inverse, near_last, part_quad, part_z = {}, {}, {}, {}, {0: dot(last[0], inverse[0])}
    for c in SIDES:
        near_centre[c] = centre(near_own[c])
        square_next[c] = kept(keep_y[c], first[c] + dot(square[c], near_centre[c])).astype(jnp.bfloat16)
        part_quad[c] = dot(inverse[0], square_next[c])
        part_z[c] = dot(last[0], inverse[c])
        near_inverse[c] = kept(near_flag[c], half(near_face[c]))
        near_quad = dot(beside([near_inverse[c], near_centre[c]]), below([square_next[0], near_next[c]]))
        near_last[c] = (-0.5 * near_quad).astype(jnp.bfloat16)
    y_total = at_once([square_next[c] for c in (0,) + SIDES], [last[0]] + [near_last[c] for c in SIDES])
    y_out[0] = y_total.astype(jnp.bfloat16)
    z_out[facing_slot[5]] = zero
    y_out[facing_slot[5]] = zero

    for c in SIDES:
        arrived(next_in, next_recv, c)
    for c in SIDES:
        last[c] = kept(keep_y[c], -0.5 * (part_quad[c] + dot(inverse[c], next_in[c]))).astype(jnp.bfloat16)
    z_total, y_part = part_z[0], {}
    for c in SIDES:
        wide = dot(last[c], beside([near_inverse[c], near_centre[c]]))
        z_total = z_total + wide[:, :BLOCK]
        z_out[slot[c]] = kept(keep_z[c], part_z[c] + wide[:, BLOCK:]).astype(jnp.bfloat16)
    y_wide = dot(square_next[0], beside([last[c] for c in SIDES]))
    y_part = {c: y_wide[:, i * BLOCK:(i + 1) * BLOCK] for i, c in enumerate(SIDES)}
    z_out[0] = z_total.astype(jnp.bfloat16)

    for c in SIDES:
        arrived(middle_in, middle_recv, c)
    for c in SIDES:
        y_out[slot[c]] = kept(keep_y[c], y_part[c] + dot(square_next[c], middle_in[c])).astype(jnp.bfloat16)

    for c in SIDES:
        @functools.partial(on_side, c)
        def _():
            part = raw.at[pl.ds(0, 2 if c == 5 else 4)]
            remote(part, part, send.at[c - 1], face_recv.at[0], place[c]).wait_send()
            z_copy(c, c).wait_send()


def store(z_in, y_in, z_out, y_out, sem):
    copies = [pltpu.make_async_copy(z_in, z_out, sem.at[0]), pltpu.make_async_copy(y_in, y_out, sem.at[1])]
    for copy in copies:
        copy.start()
    for copy in copies:
        copy.wait()


def solution(mesh):
    sizes = (mesh.shape["gx"], mesh.shape["gy"])

    def step(s_blocks, s_columns, new_home, z_pattern, y_pattern):
        any_spec = pl.BlockSpec(memory_space=pl.ANY)
        vmem = pl.BlockSpec(memory_space=pltpu.VMEM)
        buffer = pltpu.VMEM((6, BLOCK, BLOCK), jnp.bfloat16)
        single = pltpu.VMEM((BLOCK, BLOCK), jnp.bfloat16)
        dma = pltpu.SemaphoreType.DMA
        z, y = pl.pallas_call(
            lambda *refs: kernel(sizes, *refs),
            name="newton_schulz",
            out_shape=(pltpu.VMEM((7, BLOCK, BLOCK), jnp.bfloat16),) * 2,
            in_specs=[any_spec] * 5,
            out_specs=(vmem, vmem),
            scratch_shapes=[
                pltpu.VMEM((9, BLOCK, BLOCK), jnp.bfloat16),
                pltpu.SMEM((2, 1, 4), jnp.int32),
                pltpu.SMEM((1, 1), jnp.int32),
                pltpu.SMEM((6, 1, 7), jnp.int32),
                pltpu.SMEM((2, 1, 7), jnp.int32),
                buffer, single, single, single,
                buffer, buffer, buffer, buffer,
                dma((5,)), pltpu.SemaphoreType.REGULAR, dma((4,)), dma((5,)), dma((5,)), dma((2,)),
                dma((5,)), dma((4,)), dma((4,)), dma((5,)), dma((5,)),
            ],
            compiler_params=pltpu.CompilerParams(collective_id=0, has_side_effects=True),
        )(s_blocks[0], s_columns, new_home.reshape(1, 1), z_pattern, y_pattern)
        z, y = pl.pallas_call(
            store,
            name="store",
            out_shape=(jax.ShapeDtypeStruct((7, BLOCK, BLOCK), jnp.bfloat16),) * 2,
            in_specs=[any_spec] * 2,
            out_specs=(any_spec,) * 2,
            scratch_shapes=[dma((2,))],
            compiler_params=pltpu.CompilerParams(vmem_limit_bytes=1 << 20),
        )(z, y)
        return jnp.transpose(z, (1, 0, 2))[None], jnp.transpose(y, (1, 0, 2))[None]

    row = P(("gx", "gy", "gz"))
    wide = P(("gx", "gy", "gz"), None)
    block = P(("gx", "gy", "gz"), None, None, None)
    return jax.shard_map(
        step, mesh=mesh, in_specs=(block, wide, row, wide, wide), out_specs=(block, block), check_vma=False
    )
```

time: 24.2 us -> 24.3 us (level)
  no operation moved by 1% of the time
where the time goes in v3:
time: 24.3 us; the launch traced here: 24.1 us
  Pallas kernels  22.8 us (94%)
  between operations  1.28 us (5%)
    pallas_call x1, Pallas kernels, step(): pl.pallas_call(lambda *refs: kernel(sizes, *refs), name='newton_schulz',...  22 us
    pallas_call x1, Pallas kernels, step(): pl.pallas_call(store, name='store', out_shape=(jax.ShapeDtypeStruct((7, B...  0.78 us

profile of v3, /device:TPU:1, one launch (start us, length us, event | category | flops | bytes accessed | tf_op | source)
XLA Modules:
  0.0 24.1 jit_solution(9983940047740007416)
XLA Ops:
  1.3 22.0 %newton_schulz.1 = (bf16[7,128,128]{2,1,0:T(8,128)(2,1)S(1)}, bf16[7,128,128]{2,1,0:T(8,128)(2,1)S(1)}) custom-call(bf16[4,128,128]{2,1,0:T(8,128)(2,1)} %bitcast.9, s32[1,4]{1,0:T(1,128)} %refs_1_.1, s32[1,1]{1,0:T(1,128)} %bitcast.8.refs_2_, s32[1,7]{1,0:T(1,128)} %refs_3_.1, s32[1,7]{1,0:T(1,128)} %refs_4_.1), custom_call_target="tpu_custom_call" | custom-call | tf_op jit(solution)/shard_map/newton_schulz/pallas_call | solution.py:285
  23.3 0.8 %store.1 = (bf16[7,128,128]{2,1,0:T(8,128)(2,1)}, bf16[7,128,128]{2,1,0:T(8,128)(2,1)}) custom-call(bf16[7,128,128]{2,1,0:T(8,128)(2,1)S(1)} %get-tuple-element.6.z_in, bf16[7,128,128]{2,1,0:T(8,128)(2,1)S(1)} %get-tuple-element.7.y_in), custom_call_target="tpu_custom_call" | custom-call | tf_op jit(solution)/shard_map/store/pallas_call | solution.py:304

commit v4 on v3

--- a/solution.py
+++ b/solution.py
@@ -107,7 +107,6 @@
         remote(raw.at[pl.ds(0, 4)], raw.at[pl.ds(4, 4)], move.at[2], move.at[3], place[5]).start()
         moves[0].start()
         pl.semaphore_wait(barrier, sum(jnp.where(inside[c], 2, 0) for c in LINKS))
-        signal(pair_sem, place[5])
 
     for load in loads[1:]:
         load.wait()
@@ -145,16 +144,27 @@
     for c in LINKS:
         face_out[c] = raw[kept_found[c]]
 
-    @pl.when(low)
-    def _():
-        pl.semaphore_wait(pair_sem, 1)
-
-    for c in LINKS:
-        on_side(c, remote(face_out.at[c], face_in.at[FACING[c]], send.at[c - 1], face_recv.at[FACING[c] - 1], place[c]).start)
-    for c in LINKS:
-        on_side(c, remote(own_out, own_in.at[FACING[c]], send.at[c - 1], own_recv.at[FACING[c] - 1], place[c]).start)
-    for c in LINKS:
-        on_side(c, z_copy(c, FACING[c]).start)
+    def send_faces(core):
+        for c in LINKS:
+            copy = remote(
+                face_out.at[c], face_in.at[FACING[c]], send.at[c - 1], face_recv.at[FACING[c] - 1], place[c]
+            )
+            pl.when(jnp.logical_and(inside[c], core))(copy.start)
+
+    def send_owns(core):
+        for c in LINKS:
+            copy = remote(
+                own_out, own_in.at[FACING[c]], send.at[c - 1], own_recv.at[FACING[c] - 1], place[c]
+            )
+            pl.when(jnp.logical_and(inside[c], core))(copy.start)
+
+    send_faces(high)
+    send_owns(high)
+
+    @pl.when(high)
+    def _():
+        signal(pair_sem, place[5])
+
     moves[0].wait_send()
 
     for c in LINKS:
@@ -194,6 +204,15 @@
         inverse[c] = kept(keep_z[c], middle[c])
     first = {c: dot(square[0], middle[c]) for c in (0,) + SIDES}
     moves[1].wait_send()
+
+    @pl.when(low)
+    def _():
+        pl.semaphore_wait(pair_sem, 1)
+
+    send_faces(low)
+    send_owns(low)
+    for c in LINKS:
+        on_side(c, z_copy(c, FACING[c]).start)
     y_copy.wait_recv()
     near_index = pick(other_column, facing_slot[5], 4 - base)
 

time: 24.3 us -> 23.8 us (0.979)
  Pallas kernels: 22.8 us -> 22.3 us
    pallas_call x1, Pallas kernels: 22 us -> 21.5 us  [step(): pl.pallas_call(lambda *refs: kernel(sizes, *refs), name='newton_schulz',...]
where the time goes in v4:
time: 23.8 us; the launch traced here: 23.6 us
  Pallas kernels  22.3 us (94%)
  between operations  1.28 us (5%)
    pallas_call x1, Pallas kernels, step(): pl.pallas_call(lambda *refs: kernel(sizes, *refs), name='newton_schulz',...  21.5 us
    pallas_call x1, Pallas kernels, step(): pl.pallas_call(store, name='store', out_shape=(jax.ShapeDtypeStruct((7, B...  0.78 us

profile of v4, /device:TPU:1, one launch (start us, length us, event | category | flops | bytes accessed | tf_op | source)
XLA Modules:
  0.0 23.6 jit_solution(1334695585054919855)
XLA Ops:
  1.3 21.5 %newton_schulz.1 = (bf16[7,128,128]{2,1,0:T(8,128)(2,1)S(1)}, bf16[7,128,128]{2,1,0:T(8,128)(2,1)S(1)}) custom-call(bf16[4,128,128]{2,1,0:T(8,128)(2,1)} %bitcast.9, s32[1,4]{1,0:T(1,128)} %refs_1_.1, s32[1,1]{1,0:T(1,128)} %bitcast.8.refs_2_, s32[1,7]{1,0:T(1,128)} %refs_3_.1, s32[1,7]{1,0:T(1,128)} %refs_4_.1), custom_call_target="tpu_custom_call" | custom-call | tf_op jit(solution)/shard_map/newton_schulz/pallas_call | solution.py:304
  22.8 0.8 %store.1 = (bf16[7,128,128]{2,1,0:T(8,128)(2,1)}, bf16[7,128,128]{2,1,0:T(8,128)(2,1)}) custom-call(bf16[7,128,128]{2,1,0:T(8,128)(2,1)S(1)} %get-tuple-element.6.z_in, bf16[7,128,128]{2,1,0:T(8,128)(2,1)S(1)} %get-tuple-element.7.y_in), custom_call_target="tpu_custom_call" | custom-call | tf_op jit(solution)/shard_map/store/pallas_call | solution.py:323

commit v5 on v4

--- a/solution.py
+++ b/solution.py
@@ -87,8 +87,8 @@
     def _():
         pl.semaphore_wait(barrier, 1)
         signal(pair_sem, place[5])
+        moves[0].start()
         moves[1].start()
-        moves[0].start()
 
     for c in LINKS:
         @pl.when(inside[c])
@@ -176,7 +176,7 @@
                 z_keep[c, 0, i] = 0
 
     def send_to(source, target, sems):
-        for c in SIDES:
+        for c in (5,) + LINKS:
             on_side(c, remote(source, target.at[FACING[c]], send.at[c - 1], sems.at[FACING[c] - 1], place[c]).start)
 
     def arrived(buffer, sems, c):

time: 23.8 us -> 23.7 us (level)
  no operation moved by 1% of the time
where the time goes in v5:
time: 23.7 us; the launch traced here: 23.5 us
  Pallas kernels  22.2 us (94%)
  between operations  1.28 us (5%)
    pallas_call x1, Pallas kernels, step(): pl.pallas_call(lambda *refs: kernel(sizes, *refs), name='newton_schulz',...  21.4 us
    pallas_call x1, Pallas kernels, step(): pl.pallas_call(store, name='store', out_shape=(jax.ShapeDtypeStruct((7, B...  0.78 us

profile of v5, /device:TPU:1, one launch (start us, length us, event | category | flops | bytes accessed | tf_op | source)
XLA Modules:
  0.0 23.5 jit_solution(11157364784388877494)
XLA Ops:
  1.3 21.4 %newton_schulz.1 = (bf16[7,128,128]{2,1,0:T(8,128)(2,1)S(1)}, bf16[7,128,128]{2,1,0:T(8,128)(2,1)S(1)}) custom-call(bf16[4,128,128]{2,1,0:T(8,128)(2,1)} %bitcast.9, s32[1,4]{1,0:T(1,128)} %refs_1_.1, s32[1,1]{1,0:T(1,128)} %bitcast.8.refs_2_, s32[1,7]{1,0:T(1,128)} %refs_3_.1, s32[1,7]{1,0:T(1,128)} %refs_4_.1), custom_call_target="tpu_custom_call" | custom-call | tf_op jit(solution)/shard_map/newton_schulz/pallas_call | solution.py:304
  22.7 0.8 %store.1 = (bf16[7,128,128]{2,1,0:T(8,128)(2,1)}, bf16[7,128,128]{2,1,0:T(8,128)(2,1)}) custom-call(bf16[7,128,128]{2,1,0:T(8,128)(2,1)S(1)} %get-tuple-element.6.z_in, bf16[7,128,128]{2,1,0:T(8,128)(2,1)S(1)} %get-tuple-element.7.y_in), custom_call_target="tpu_custom_call" | custom-call | tf_op jit(solution)/shard_map/store/pallas_call | solution.py:323
